TPU v7x, 32 devices: a whole 2x2x4 slice. The times are simulated.
32 devices in a mesh: role: 2 (over y), tile: 16 (over z, x, core).
Axes of the slice: x: 2, y: 2, z: 4, core: 2. Of those that a mesh axis runs over, the one named last changes fastest.
Arguments:
- fields_pair: float32 [2, 512, 16384], P('role', None, 'tile'), may hold values from 0 to 1
- velocity: float32 [16384], P('tile'), may hold values from -0.5 to 0.5
- growth: float32 [16384], P('tile'), may hold values from 0.05 to 0.5
- features: bfloat16 [512, 1024], replicated, may hold values from -6 to 6
- assignment: int32 [512], replicated, may hold values from 0 to 511, each once
- out_pair: float32 [2, 1024, 16384], P('role', None, 'tile'), may hold values from -0.1875 to 0.1875
- hidden_pair: float32 [2, 5, 1024, 1024], P('role', None, 'tile'), may hold values from -0.1875 to 0.1875
Outputs:
- fields_next: float32 [2, 512, 16384], P('role', None, 'tile')
- out_next: float32 [2, 1024, 16384], P('role', None, 'tile')
- hidden_next: float32 [2, 5, 1024, 1024], P('role', None, 'tile')
Inputs may be any that keep to these rules, and one draw needn't show every extreme that they name: `assignment`: a permutation of the 512 members.
All inputs are finite; a program needn't handle non-finite values.
Results may differ from a plain program's by a relative error of at most 0.0022.
The roundings to bfloat16 on the way count: a program that leaves them out, or rounds other values in their place, can miss the bound.
Values may be sent and summed in bfloat16 or wider, within the bound.
A program may use at most 192 MiB of HBM per device.

v0:
```python
import jax
import jax.numpy as jnp
from jax import lax
from jax.sharding import PartitionSpec as P

momentum_decay = 0.9
step_size = 0.1


def extended(value, axis, dim, width):
    count, length = (lax.axis_size(axis), value.shape[dim])
    up = [(i, (i + 1) % count) for i in range(count)]
    down = [(j, i) for i, j in up]
    last = lax.slice_in_dim(value, length - width, length, axis=dim)
    leading = lax.slice_in_dim(value, 0, width, axis=dim)
    before = lax.ppermute(last, axis, up)
    after = lax.ppermute(leading, axis, down)
    return jnp.concatenate([before, value, after], axis=dim)


def silu_slope(values):
    logistic = jax.nn.sigmoid(values)
    return logistic * (1.0 + values * (1.0 - logistic))


def advance(padded, growth):
    states = padded[:-1]
    velocity_row = padded[-1]
    outflow = (
        jnp.maximum(velocity_row[:-1], 0.0) * states[:, :-1]
        + jnp.minimum(velocity_row[:-1], 0.0) * states[:, 1:]
    )
    carried = states[:, 1:-1] - outflow[:, 1:] + outflow[:, :-1]
    return carried + growth * carried * (1.0 - carried)


def to_trainer(value):
    return lax.ppermute(value.astype(jnp.bfloat16), "role", [(0, 1)])


def to_solver(value):
    return lax.ppermute(value.astype(jnp.bfloat16), "role", [(1, 0)])


def plain_training(features, hidden_narrow, out_narrow, own_fields, own_out, own_hidden):
    layer_count, unit_rows = own_hidden.shape[:2]
    batch = own_fields.shape[0]
    first_unit = lax.axis_index("tile") * unit_rows
    momentum_out = to_trainer(own_out)
    momentum_hidden = to_trainer(own_hidden)
    full_hidden = [
        lax.all_gather(hidden_narrow[i], "tile", axis=0, tiled=True) for i in range(layer_count)
    ]
    inputs, summed_list = ([], [])
    activation = features
    for i in range(layer_count):
        inputs.append(activation)
        summed = jnp.dot(activation, full_hidden[i], preferred_element_type=jnp.float32)
        summed_list.append(summed)
        activation = jax.nn.silu(summed).astype(jnp.bfloat16)
    predicted = jnp.dot(activation, out_narrow, preferred_element_type=jnp.float32)
    residual = ((predicted - own_fields) / batch).astype(jnp.bfloat16)
    partial_grad = lax.dot_general(
        residual, out_narrow, (((1,), (1,)), ((), ())), preferred_element_type=jnp.float32
    )
    upstream = lax.psum(partial_grad, "tile")
    grad_out = jnp.dot(activation.T, residual, preferred_element_type=jnp.float32)
    sent_out = to_solver(grad_out)
    gradients, sent = ([], [])
    for i in reversed(range(layer_count)):
        slope = (upstream * silu_slope(summed_list[i])).astype(jnp.bfloat16)
        own_inputs = lax.dynamic_slice_in_dim(inputs[i], first_unit, unit_rows, 1)
        gradient = jnp.dot(own_inputs.T, slope, preferred_element_type=jnp.float32)
        gradients.append(gradient)
        sent.append(to_solver(gradient))
        if i > 0:
            upstream = lax.dot_general(
                slope, full_hidden[i], (((1,), (1,)), ((), ())), preferred_element_type=jnp.float32
            )
    solver_side = lax.axis_index("role") == 0
    other_out = jnp.where(solver_side, sent_out, momentum_out)
    other_hidden = jnp.where(solver_side, jnp.stack(sent[::-1]), momentum_hidden)
    return (grad_out, jnp.stack(gradients[::-1]), other_out, other_hidden)


def body(fields_pair, velocity, growth, features, assignment, out_pair, hidden_pair):
    solver_side = lax.axis_index("role") == 0
    own_fields = fields_pair[0]
    own_out = out_pair[0]
    own_hidden = hidden_pair[0]
    stacked = jnp.concatenate([own_fields, velocity[None, :]], axis=0)
    advanced = advance(extended(stacked, "tile", 1, 1), growth)
    fresh_fields = to_trainer(advanced)
    grad_out, grad_hidden, other_out, other_hidden = plain_training(
        features,
        own_hidden.astype(jnp.bfloat16),
        own_out.astype(jnp.bfloat16),
        own_fields,
        own_out,
        own_hidden,
    )
    grad_out, grad_hidden, other_out, other_hidden = (
        v.astype(jnp.float32) for v in (grad_out, grad_hidden, other_out, other_hidden)
    )
    out_next = jnp.where(
        solver_side,
        momentum_decay * own_out + other_out,
        own_out - step_size * (momentum_decay * other_out + grad_out),
    )
    hidden_next = jnp.where(
        solver_side,
        momentum_decay * own_hidden + other_hidden,
        own_hidden - step_size * (momentum_decay * other_hidden + grad_hidden),
    )
    next_batch = jnp.take(fresh_fields, assignment, axis=0).astype(jnp.float32)
    fields_next = jnp.where(solver_side, advanced, next_batch)
    return (fields_next[None], out_next[None], hidden_next[None])


def solution(mesh):
    return jax.shard_map(
        body,
        mesh=mesh,
        in_specs=(
            P("role", None, "tile"),
            P("tile"),
            P("tile"),
            P(),
            P(),
            P("role", None, "tile"),
            P("role", None, "tile", None),
        ),
        out_specs=(P("role", None, "tile"), P("role", None, "tile"), P("role", None, "tile", None)),
        check_vma=False,
    )
```

profile of v0, /device:TPU:0, one launch (start us, length us, event | category | flops | bytes accessed | tf_op | source)
XLA Modules:
  0.0 390.6 jit_solution(13564146009136946338)
XLA Ops:
  7.2 1.5 bitcast_convert_fusion.1
  8.7 0.8 copy-done.6
  9.5 0.8 fusion.60
  13.1 5.9 %collective-permute-start.10 = (bf16[5,64,1024]{2,1,0:T(8,128)(2,1)}, bf16[5,64,1024]{2,1,0:T(8,128)(2,1)}, u32[]{:S(2)}, u32[]{:S(2)}) collective-permute-start(bf16[5,64,1024]{2,1,0:T(8,128)(2,1)} %copy-done.6), channel_id=1, source_target_pairs={{0,16},{1,17},{2,18},{3,19},{4,20},{5,21},{6,22},{7,23},{8,24},{9,... | collective-permute-start | bytes 1966088 | tf_op jit(solution)/shard_map/ppermute | solution.py:38
  19.0 4.0 %bitcast_convert_fusion = bf16[1024,1024]{1,0:T(8,128)(2,1)} fusion(f32[1,1024,1024]{2,1,0:T(8,128)} %param.12), kind=kLoop, calls=%fused_computation.8 | loop fusion | flops 1048576 | bytes 6291456 | tf_op jit(solution)/shard_map/convert_element_type | solution.py:97
  23.0 2.8 collective-permute-start.4
  26.0 4.4 %collective-permute-start.1 = (f32[513,1]{1,0:T(8,128)S(1)}, f32[513,1]{1,0:T(8,128)S(1)}, u32[]{:S(2)}, u32[]{:S(2)}) collective-permute-start(f32[513,1]{1,0:T(8,128)S(1)} %get-tuple-element.8), channel_id=1, source_target_pairs={{1,0},{2,1},{3,2},{4,3},{5,4},{6,5},{7,6},{8,7},{9,8},{10,9},{11,1... | collective-permute-start | bytes 6164 | tf_op jit(solution)/shard_map/ppermute | solution.py:17
  30.4 5.4 %collective-permute-done = f32[513,1]{1,0:T(8,128)S(1)} collective-permute-done((f32[513,1]{1,0:T(8,128)S(1)}, f32[513,1]{1,0:T(8,128)S(1)}, u32[]{:S(2)}, u32[]{:S(2)}) %collective-permute-start) | collective-permute-done | bytes 2084 | tf_op jit(solution)/shard_map/ppermute | solution.py:16
  36.7 2.4 fusion.59
  39.1 1.5 collective-permute-start.2
  40.6 15.2 %all-gather.11.cloned.1.call-done = bf16[1,1024,1024]{2,1,0:T(8,128)(2,1)} async-done(((bf16[1,64,1024]{2,1,0:T(8,128)(2,1)}), bf16[1,1024,1024]{2,1,0:T(8,128)(2,1)}) %all-gather.11.cloned.1.call-update) | async-done | bytes 2097168 | tf_op jit(solution)/shard_map/all_gather | solution.py:52
  55.8 4.6 %multiply_convert_fusion.10 = (bf16[512,1024]{1,0:T(8,128)(2,1)}, f32[512,1024]{1,0:T(8,128)}) fusion(bf16[512,1024]{1,0:T(8,128)(2,1)S(1)} %copy-done, bf16[1,1024,1024]{2,1,0:T(8,128)(2,1)} %all-gather.11.cloned.1.call-done), kind=kOutput, calls=%fused_computation.51 | convolution fusion | flops 1076363264 | bytes 6291456 | tf_op jit(solution)/shard_map/dot_general | solution.py:58
  60.5 37.8 %all-gather.13.cloned.1.call-done = bf16[1,1024,1024]{2,1,0:T(8,128)(2,1)} async-done(((bf16[1,64,1024]{2,1,0:T(8,128)(2,1)}), bf16[1,1024,1024]{2,1,0:T(8,128)(2,1)}) %all-gather.13.cloned.1.call-update) | async-done | bytes 2097168 | tf_op jit(solution)/shard_map/all_gather | solution.py:52
  98.2 4.7 %multiply_convert_fusion.9 = (bf16[512,1024]{1,0:T(8,128)(2,1)S(1)}, f32[512,1024]{1,0:T(8,128)}) fusion(bf16[512,1024]{1,0:T(8,128)(2,1)} %get-tuple-element.14, bf16[1,1024,1024]{2,1,0:T(8,128)(2,1)} %all-gather.13.cloned.1.call-done), kind=kOutput, calls=%fused_computation.49 | convolution fusion | flops 1076363264 | bytes 6291456 | tf_op jit(solution)/shard_map/dot_general | solution.py:58
  102.9 37.7 %all-gather.15.cloned.1.call-done = bf16[1,1024,1024]{2,1,0:T(8,128)(2,1)} async-done(((bf16[1,64,1024]{2,1,0:T(8,128)(2,1)}), bf16[1,1024,1024]{2,1,0:T(8,128)(2,1)}) %all-gather.15.cloned.1.call-update) | async-done | bytes 2097168 | tf_op jit(solution)/shard_map/all_gather | solution.py:52
  140.6 4.7 %multiply_convert_fusion.8 = (bf16[512,1024]{1,0:T(8,128)(2,1)}, f32[512,1024]{1,0:T(8,128)}) fusion(bf16[512,1024]{1,0:T(8,128)(2,1)S(1)} %get-tuple-element.16, bf16[1,1024,1024]{2,1,0:T(8,128)(2,1)} %all-gather.15.cloned.1.call-done), kind=kOutput, calls=%fused_computation.47 | convolution fusion | flops 1076363264 | bytes 6291456 | tf_op jit(solution)/shard_map/dot_general | solution.py:58
  145.3 37.5 %all-gather.17.cloned.1.call-done = bf16[1,1024,1024]{2,1,0:T(8,128)(2,1)} async-done(((bf16[1,64,1024]{2,1,0:T(8,128)(2,1)}), bf16[1,1024,1024]{2,1,0:T(8,128)(2,1)}) %all-gather.17.cloned.1.call-update) | async-done | bytes 2097168 | tf_op jit(solution)/shard_map/all_gather | solution.py:52
  182.8 4.7 %multiply_convert_fusion.7 = (bf16[512,1024]{1,0:T(8,128)(2,1)S(1)}, f32[512,1024]{1,0:T(8,128)}) fusion(bf16[512,1024]{1,0:T(8,128)(2,1)} %get-tuple-element.18, bf16[1,1024,1024]{2,1,0:T(8,128)(2,1)} %all-gather.17.cloned.1.call-done), kind=kOutput, calls=%fused_computation.45 | convolution fusion | flops 1076363264 | bytes 6291456 | tf_op jit(solution)/shard_map/dot_general | solution.py:58
  187.6 38.1 %all-gather.19.cloned.1.call-done = bf16[1,1024,1024]{2,1,0:T(8,128)(2,1)} async-done(((bf16[1,64,1024]{2,1,0:T(8,128)(2,1)}), bf16[1,1024,1024]{2,1,0:T(8,128)(2,1)}) %all-gather.19.cloned.1.call-update) | async-done | bytes 2097168 | tf_op jit(solution)/shard_map/all_gather | solution.py:52
  225.6 3.0 fusion.10
  228.7 3.7 multiply_convert_fusion.5
  232.3 1.0 copy-done.19
  233.3 4.2 %fusion.64 = f32[512,1024]{1,0:T(8,128)} fusion(bf16[512,1024]{1,0:T(8,128)(2,1)S(1)} %multiply_convert_fusion.5, bf16[1024,1024]{1,0:T(8,128)(2,1)} %bitcast_convert_fusion), kind=kOutput, calls=%fused_computation.103 | convolution fusion | flops 1073741824 | bytes 5242880 | tf_op jit(solution)/shard_map/dot_general | solution.py:63
  237.6 2.1 gather_fusion
  239.6 3.4 select_bitcast_fusion
  243.0 4.1 %fusion.61 = (bf16[1024,1024]{1,0:T(8,128)(2,1)}, f32[1024,1024]{1,0:T(8,128)}) fusion(bf16[512,1024]{1,0:T(8,128)(2,1)S(1)} %copy-done.20, f32[512,1024]{1,0:T(8,128)S(1)} %copy-done.8), kind=kOutput, calls=%fused_computation.102 | convolution fusion | flops 1077411840 | bytes 9437184 | tf_op jit(solution)/shard_map/dot_general | solution.py:67
  247.1 1.5 collective-permute-start.3
  248.6 86.0 %all-reduce.2.cloned.1.call-done = f32[512,1024]{1,0:T(8,128)} async-done(((f32[512,1024]{1,0:T(8,128)}), f32[512,1024]{1,0:T(8,128)}) %all-reduce.2.cloned.1.call-update) | async-done | bytes 2097168 | tf_op jit(solution)/shard_map/psum | solution.py:66
  334.6 3.0 multiply_convert_fusion.4
  337.5 4.0 %multiply_convert_fusion.3 = bf16[512,1024]{1,0:T(8,128)(2,1)S(1)} fusion(f32[512,1024]{1,0:T(8,128)} %get-tuple-element.21, bf16[512,1024]{1,0:T(8,128)(2,1)S(1)} %multiply_convert_fusion.4, bf16[1,1024,1024]{2,1,0:T(8,128)(2,1)} %all-gather.19.cloned.1.call-done), kind=kOutput, calls=%fused_computation.40 | convolution fusion | flops 1078460416 | bytes 6291456 | tf_op jit(solution)/shard_map/dot_general | solution.py:77
  341.6 1.6 multiply_convert_fusion.2
  344.1 2.6 multiply_convert_fusion.1
  346.7 4.3 %bitcast_dynamic-update-slice_fusion.4 = (f32[5,64,1024]{2,1,0:T(8,128)S(1)}, bf16[64,1024]{1,0:T(8,128)(2,1)S(1)}) fusion(f32[512,1024]{1,0:T(8,128)} %get-tuple-element.15, bf16[512,1024]{1,0:T(8,128)(2,1)} %multiply_convert_fusion.1, bf16[1,1024,1024]{2,1,0:T(8,128)(2,1)} %all-gather.13.cloned.1.call-done, bf16[512,1024]{1,0:T(8,128)(2,1)S(1)} %copy-done, ...), kind=kOutput, calls=%fused_computation.72 | convolution fusion | flops 1145634816 | bytes 5767172 | tf_op jit(solution)/shard_map/dot_general | solution.py:73
  351.1 1.8 bitcast_dynamic-update-slice_fusion.3
  352.9 1.3 collective-permute-start.6
  354.2 1.3 collective-permute-start.5
  355.5 1.7 bitcast_dynamic-update-slice_fusion.2
  357.2 1.5 bitcast_dynamic-update-slice_fusion.1
  358.7 1.5 bitcast_dynamic-update-slice_fusion
  360.2 1.8 collective-permute-done.5
  362.0 1.3 collective-permute-start.7
  363.3 1.3 collective-permute-start.8
  364.6 4.2 %collective-permute-done.7 = bf16[64,1024]{1,0:T(8,128)(2,1)S(1)} collective-permute-done((bf16[64,1024]{1,0:T(8,128)(2,1)S(1)}, bf16[64,1024]{1,0:T(8,128)(2,1)S(1)}, u32[]{:S(2)}, u32[]{:S(2)}) %collective-permute-start.7) | collective-permute-done | bytes 131104 | tf_op jit(solution)/shard_map/ppermute | solution.py:42
  368.8 1.3 collective-permute-start.9
  370.2 5.4 %collective-permute-done.9 = bf16[64,1024]{1,0:T(8,128)(2,1)S(1)} collective-permute-done((bf16[64,1024]{1,0:T(8,128)(2,1)S(1)}, bf16[64,1024]{1,0:T(8,128)(2,1)S(1)}, u32[]{:S(2)}, u32[]{:S(2)}) %collective-permute-start.9) | collective-permute-done | bytes 131104 | tf_op jit(solution)/shard_map/ppermute | solution.py:42
  375.7 1.6 fusion.35
  377.3 1.1 copy-done.3
  378.4 5.3 %fusion.1 = f32[1,1024,1024]{2,1,0:T(8,128)} fusion(f32[1024,1024]{1,0:T(8,128)S(1)} %copy-done.5, f32[1,1024,1024]{2,1,0:T(8,128)S(1)} %copy-done.3, bf16[1024,1024]{1,0:T(8,128)(2,1)} %collective-permute-done.3, bf16[1024,1024]{1,0:T(8,128)(2,1)} %collective-permute-done.4, pred[]{:T(512)S(6)} %eq.4), kind=kLoop, calls=%fused_computation.4 | loop fusion | flops 9437184 | bytes 16777216 | tf_op jit(solution)/shard_map/broadcast_in_dim | solution.py:117
  (74 shorter events, 4.9 us)
Async XLA Ops:
  7.2 48.7 %copy-start = (bf16[512,1024]{1,0:T(8,128)(2,1)S(1)}, bf16[512,1024]{1,0:T(8,128)(2,1)}, u32[]{:S(2)}) copy-start(bf16[512,1024]{1,0:T(8,128)(2,1)} %param.10) | copy-start | bytes 3145732
  7.2 48.7 %all-gather.11.cloned.1.call-start = ((), (), s32[]{:S(2)}) async-start(), calls=%async_computation.1 | async-start | bytes 2228224 | tf_op jit(solution)/shard_map/all_gather | solution.py:52
  8.7 0.8 copy-start.6
  10.4 87.8 %all-gather.13.cloned.1.call-start = ((), (), s32[]{:S(2)}) async-start(), calls=%async_computation.2 | async-start | bytes 2228224 | tf_op jit(solution)/shard_map/all_gather | solution.py:52
  11.2 129.5 %all-gather.15.cloned.1.call-start = ((), (), s32[]{:S(2)}) async-start(), calls=%async_computation.3 | async-start | bytes 2228224 | tf_op jit(solution)/shard_map/all_gather | solution.py:52
  11.9 170.9 %all-gather.17.cloned.1.call-start = ((), (), s32[]{:S(2)}) async-start(), calls=%async_computation.4 | async-start | bytes 2228224 | tf_op jit(solution)/shard_map/all_gather | solution.py:52
  12.5 213.2 %all-gather.19.cloned.1.call-start = ((), (), s32[]{:S(2)}) async-start(), calls=%async_computation.5 | async-start | bytes 2228224 | tf_op jit(solution)/shard_map/all_gather | solution.py:52
  13.1 12.7 %copy-start.1 = (f32[1,512,1024]{2,1,0:T(8,128)S(1)}, f32[1,512,1024]{2,1,0:T(8,128)}, u32[]{:S(2)}) copy-start(f32[1,512,1024]{2,1,0:T(8,128)} %param.7) | copy-start | bytes 6291460
  13.1 12.7 %copy-start.12 = (f32[1024]{0:T(1024)S(1)}, f32[1024]{0:T(1024)}, u32[]{:S(2)}) copy-start(f32[1024]{0:T(1024)} %param.8) | copy-start | bytes 12292
  13.1 321.5 %all-reduce.2.cloned.1.call-start = ((), (), s32[]{:S(2)}) async-start(), calls=%async_computation | async-start | bytes 4194304 | tf_op jit(solution)/shard_map/psum | solution.py:66
  13.1 362.6 %collective-permute-start.10 = (bf16[5,64,1024]{2,1,0:T(8,128)(2,1)}, bf16[5,64,1024]{2,1,0:T(8,128)(2,1)}, u32[]{:S(2)}, u32[]{:S(2)}) collective-permute-start(bf16[5,64,1024]{2,1,0:T(8,128)(2,1)} %copy-done.6), channel_id=1, source_target_pairs={{0,16},{1,17},{2,18},{3,19},{4,20},{5,21},{6,22},{7,23},{8,24},{9,... | collective-permute-start | bytes 1966088 | tf_op jit(solution)/shard_map/ppermute | solution.py:38
  23.0 7.4 %copy-start.15 = (s32[512]{0:T(512)S(1)}, s32[512]{0:T(512)}, u32[]{:S(2)}) copy-start(s32[512]{0:T(512)} %param.11) | copy-start | bytes 6148
  23.0 354.3 %collective-permute-start.4 = (bf16[1024,1024]{1,0:T(8,128)(2,1)}, bf16[1024,1024]{1,0:T(8,128)(2,1)}, u32[]{:S(2)}, u32[]{:S(2)}) collective-permute-start(bf16[1024,1024]{1,0:T(8,128)(2,1)} %bitcast_convert_fusion), channel_id=1, source_target_pairs={{0,16},{1,17},{2,18},{3,19},{4,20},{5,21},{6,22},{7,23},{8,24},{9,... | collective-permute-start | bytes 6291464 | tf_op jit(solution)/shard_map/ppermute | solution.py:38
  25.9 9.9 %collective-permute-start = (f32[513,1]{1,0:T(8,128)S(1)}, f32[513,1]{1,0:T(8,128)S(1)}, u32[]{:S(2)}, u32[]{:S(2)}) collective-permute-start(f32[513,1]{1,0:T(8,128)S(1)} %get-tuple-element.7), channel_id=1, source_target_pairs={{0,1},{1,2},{2,3},{3,4},{4,5},{5,6},{6,7},{7,8},{8,9},{9,10},{10,1... | collective-permute-start | bytes 6164 | tf_op jit(solution)/shard_map/ppermute | solution.py:16
  26.0 10.0 %collective-permute-start.1 = (f32[513,1]{1,0:T(8,128)S(1)}, f32[513,1]{1,0:T(8,128)S(1)}, u32[]{:S(2)}, u32[]{:S(2)}) collective-permute-start(f32[513,1]{1,0:T(8,128)S(1)} %get-tuple-element.8), channel_id=1, source_target_pairs={{1,0},{2,1},{3,2},{4,3},{5,4},{6,5},{7,6},{8,7},{9,8},{10,9},{11,1... | collective-permute-start | bytes 6164 | tf_op jit(solution)/shard_map/ppermute | solution.py:17
  35.9 0.7 copy-start.16
  39.1 198.5 %collective-permute-start.2 = (bf16[512,1024]{1,0:T(8,128)(2,1)}, bf16[512,1024]{1,0:T(8,128)(2,1)S(1)}, u32[]{:S(2)}, u32[]{:S(2)}) collective-permute-start(bf16[512,1024]{1,0:T(8,128)(2,1)} %get-tuple-element.5), channel_id=1, source_target_pairs={{0,16},{1,17},{2,18},{3,19},{4,20},{5,21},{6,22},{7,23},{8,24},{9,... | collective-permute-start | bytes 3145736 | tf_op jit(solution)/shard_map/ppermute | solution.py:38
  102.9 42.4 %copy-start.13 = (bf16[512,1024]{1,0:T(8,128)(2,1)}, bf16[512,1024]{1,0:T(8,128)(2,1)S(1)}, u32[]{:S(2)}) copy-start(bf16[512,1024]{1,0:T(8,128)(2,1)S(1)} %get-tuple-element.16) | copy-start | bytes 3145732
  187.5 41.1 %copy-start.14 = (bf16[512,1024]{1,0:T(8,128)(2,1)}, bf16[512,1024]{1,0:T(8,128)(2,1)S(1)}, u32[]{:S(2)}) copy-start(bf16[512,1024]{1,0:T(8,128)(2,1)S(1)} %get-tuple-element.20) | copy-start | bytes 3145732
  225.6 3.0 copy-start.2
  228.6 3.7 copy-start.7
  232.3 1.0 copy-start.19
  239.6 3.4 copy-start.8
  239.6 3.4 copy-start.20
  247.1 130.3 %collective-permute-start.3 = (bf16[1024,1024]{1,0:T(8,128)(2,1)}, bf16[1024,1024]{1,0:T(8,128)(2,1)}, u32[]{:S(2)}, u32[]{:S(2)}) collective-permute-start(bf16[1024,1024]{1,0:T(8,128)(2,1)} %get-tuple-element.22), channel_id=1, source_target_pairs={{16,0},{17,1},{18,2},{19,3},{20,4},{21,5},{22,6},{23,7},{24,8},{25... | collective-permute-start | bytes 6291464 | tf_op jit(solution)/shard_map/ppermute | solution.py:42
  337.5 4.0 %copy-start.18 = (bf16[1,1024,1024]{2,1,0:T(8,128)(2,1)S(1)}, bf16[1,1024,1024]{2,1,0:T(8,128)(2,1)}, u32[]{:S(2)}) copy-start(bf16[1,1024,1024]{2,1,0:T(8,128)(2,1)} %all-gather.17.cloned.1.call-done) | copy-start | bytes 6291460
  337.5 4.0 %copy-start.22 = (f32[512,1024]{1,0:T(8,128)S(1)}, f32[512,1024]{1,0:T(8,128)}, u32[]{:S(2)}) copy-start(f32[512,1024]{1,0:T(8,128)} %get-tuple-element.19) | copy-start | bytes 6291460
  341.5 1.7 copy-start.9
  341.5 2.0 copy-start.17
  341.5 2.6 copy-start.21
  343.2 3.5 copy-start.11
  351.1 6.1 %copy-start.10 = (bf16[512,1024]{1,0:T(8,128)(2,1)S(1)}, bf16[512,1024]{1,0:T(8,128)(2,1)}, u32[]{:S(2)}) copy-start(bf16[512,1024]{1,0:T(8,128)(2,1)} %copy-done.9) | copy-start | bytes 3145732
  352.9 10.4 %collective-permute-start.6 = (bf16[64,1024]{1,0:T(8,128)(2,1)S(1)}, bf16[64,1024]{1,0:T(8,128)(2,1)S(1)}, u32[]{:S(2)}, u32[]{:S(2)}) collective-permute-start(bf16[64,1024]{1,0:T(8,128)(2,1)S(1)} %get-tuple-element.27), channel_id=1, source_target_pairs={{16,0},{17,1},{18,2},{19,3},{20,4},{21,5},{22,6},{23,7},{24,8},{25... | collective-permute-start | bytes 393224 | tf_op jit(solution)/shard_map/ppermute | solution.py:42
  354.2 7.8 %collective-permute-start.5 = (bf16[64,1024]{1,0:T(8,128)(2,1)S(1)}, bf16[64,1024]{1,0:T(8,128)(2,1)S(1)}, u32[]{:S(2)}, u32[]{:S(2)}) collective-permute-start(bf16[64,1024]{1,0:T(8,128)(2,1)S(1)} %get-tuple-element.25), channel_id=1, source_target_pairs={{16,0},{17,1},{18,2},{19,3},{20,4},{21,5},{22,6},{23,7},{24,8},{25... | collective-permute-start | bytes 393224 | tf_op jit(solution)/shard_map/ppermute | solution.py:42
  357.2 18.5 %copy-start.4 = (f32[1,5,64,1024]{3,2,1,0:T(8,128)S(1)}, f32[1,5,64,1024]{3,2,1,0:T(8,128)}, u32[]{:S(2)}) copy-start(f32[1,5,64,1024]{3,2,1,0:T(8,128)} %param.13) | copy-start | bytes 3932164
  357.2 20.1 %copy-start.5 = (f32[1024,1024]{1,0:T(8,128)S(1)}, f32[1024,1024]{1,0:T(8,128)}, u32[]{:S(2)}) copy-start(f32[1024,1024]{1,0:T(8,128)} %get-tuple-element.23) | copy-start | bytes 12582916
  362.0 6.8 %collective-permute-start.7 = (bf16[64,1024]{1,0:T(8,128)(2,1)S(1)}, bf16[64,1024]{1,0:T(8,128)(2,1)S(1)}, u32[]{:S(2)}, u32[]{:S(2)}) collective-permute-start(bf16[64,1024]{1,0:T(8,128)(2,1)S(1)} %get-tuple-element.29), channel_id=1, source_target_pairs={{16,0},{17,1},{18,2},{19,3},{20,4},{21,5},{22,6},{23,7},{24,8},{25... | collective-permute-start | bytes 393224 | tf_op jit(solution)/shard_map/ppermute | solution.py:42
  363.3 6.9 %collective-permute-start.8 = (bf16[64,1024]{1,0:T(8,128)(2,1)S(1)}, bf16[64,1024]{1,0:T(8,128)(2,1)S(1)}, u32[]{:S(2)}, u32[]{:S(2)}) collective-permute-start(bf16[64,1024]{1,0:T(8,128)(2,1)S(1)} %get-tuple-element.31), channel_id=1, source_target_pairs={{16,0},{17,1},{18,2},{19,3},{20,4},{21,5},{22,6},{23,7},{24,8},{25... | collective-permute-start | bytes 393224 | tf_op jit(solution)/shard_map/ppermute | solution.py:42
  368.8 6.8 %collective-permute-start.9 = (bf16[64,1024]{1,0:T(8,128)(2,1)S(1)}, bf16[64,1024]{1,0:T(8,128)(2,1)S(1)}, u32[]{:S(2)}, u32[]{:S(2)}) collective-permute-start(bf16[64,1024]{1,0:T(8,128)(2,1)S(1)} %get-tuple-element.33), channel_id=1, source_target_pairs={{16,0},{17,1},{18,2},{19,3},{20,4},{21,5},{22,6},{23,7},{24,8},{25... | collective-permute-start | bytes 393224 | tf_op jit(solution)/shard_map/ppermute | solution.py:42
  375.7 2.7 copy-start.3
Sparse Core Ops, SparseCore 0:
  10.5 45.2 all-gather.10
  58.0 40.1 all-gather.12
  100.4 40.1 all-gather.14
  142.6 40.1 all-gather.16
  185.4 40.1 all-gather.18
  237.6 96.8 all-reduce.1
where the time goes:
time: 391 us
  waiting for transfers between devices  272 us (70%)
  matrix products  52.6 us (13%)
  starting transfers between devices  22.9 us (6%)
  other arithmetic  22 us (6%)
  between operations  14.6 us (4%)
  local copies, waits for them, and re-layouts  6.81 us (2%)
    all_gather x5, waiting for transfers between devices, plain_training(): lax.all_gather(hidden_narrow[i], 'tile', axis=0, tiled=True)  166 us
    psum x1, waiting for transfers between devices, plain_training(): upstream = lax.psum(partial_grad, 'tile')  86 us
    dot_general x5, matrix products, plain_training(): jnp.dot(activation, full_hidden[i], preferred_element_type=jnp.float32)  21.8 us
    ppermute x6, waiting for transfers between devices, to_solver(): return lax.ppermute(value.astype(jnp.bfloat16), 'role', [(1, 0)])  11.5 us
    dot_general x5, matrix products, plain_training(): gradient = jnp.dot(own_inputs.T, slope, preferred_element_type=jnp.float32)  10.8 us
    broadcast_in_dim x3, other arithmetic, body(): return (fields_next[None], out_next[None], hidden_next[None])  10.3 us
    ppermute x3, starting transfers between devices, to_trainer(): return lax.ppermute(value.astype(jnp.bfloat16), 'role', [(0, 1)])  10.2 us
    dot_general x3, matrix products, plain_training(): lax.dot_general(slope, full_hidden[i], (((1,), (1,)), ((), ())), preferre...  8.2 us
  transfers between devices with their start and end apart: 17, of which 11 were waited for; matrix products, arithmetic and copies ran while one was open for 18% of the time, Pallas kernels for 0%

commit v1 on v0

--- a/solution.py
+++ b/solution.py
@@ -63,7 +63,11 @@
     partial_grad = lax.dot_general(
         residual, out_narrow, (((1,), (1,)), ((), ())), preferred_element_type=jnp.float32
     )
-    upstream = lax.psum(partial_grad, "tile")
+    upstream = partial_grad
+    for hop in (1, 2, 4, 8):
+        upstream = upstream + lax.ppermute(
+            upstream, "tile", [(dev, dev ^ hop) for dev in range(16)]
+        )
     grad_out = jnp.dot(activation.T, residual, preferred_element_type=jnp.float32)
     sent_out = to_solver(grad_out)
     gradients, sent = ([], [])

time: 391 us -> 475 us (1.21)
  waiting for transfers between devices: 272 us -> 353 us
  matrix products: 52.6 us -> 47.4 us
    ppermute x0 -> x4, waiting for transfers between devices: none -> 100 us  [plain_training(): lax.ppermute(upstream, 'tile', [(dev, dev ^ hop) for dev in range(16)])]
    psum x1 -> x0, waiting for transfers between devices: 86 us -> none  [plain_training(): upstream = lax.psum(partial_grad, 'tile')]
    ppermute x1, waiting for transfers between devices: 5.41 us -> 40.6 us  [extended(): before = lax.ppermute(last, axis, up)]
    all_gather x5, waiting for transfers between devices: 166 us -> 191 us  [plain_training(): lax.all_gather(hidden_narrow[i], 'tile', axis=0, tiled=True)]
    ppermute x3, waiting for transfers between devices: 0.01 us -> 11 us  [to_trainer(): return lax.ppermute(value.astype(jnp.bfloat16), 'role', [(0, 1)])]
  transfers between devices with their start and end apart: 17 -> 20, of which waited for: 11 -> 14; matrix products, arithmetic and copies ran while one was open for 18% -> 13% of each run, Pallas kernels for 0% -> 0%
where the time goes in v1:
time: 475 us; the launch traced here: 473 us
  waiting for transfers between devices  353 us (74%)
  matrix products  47.4 us (10%)
  other arithmetic  26.7 us (6%)
  starting transfers between devices  26.5 us (6%)
  between operations  14.2 us (3%)
  local copies, waits for them, and re-layouts  5.25 us (1%)
    all_gather x5, waiting for transfers between devices, plain_training(): lax.all_gather(hidden_narrow[i], 'tile', axis=0, tiled=True)  191 us
    ppermute x4, waiting for transfers between devices, plain_training(): lax.ppermute(upstream, 'tile', [(dev, dev ^ hop) for dev in range(16)])  100 us
    ppermute x1, waiting for transfers between devices, extended(): before = lax.ppermute(last, axis, up)  40.6 us
    dot_general x5, matrix products, plain_training(): jnp.dot(activation, full_hidden[i], preferred_element_type=jnp.float32)  20.4 us
    ppermute x3, starting transfers between devices, to_trainer(): return lax.ppermute(value.astype(jnp.bfloat16), 'role', [(0, 1)])  13 us
    broadcast_in_dim x3, other arithmetic, body(): return (fields_next[None], out_next[None], hidden_next[None])  11.6 us
    ppermute x3, waiting for transfers between devices, to_trainer(): return lax.ppermute(value.astype(jnp.bfloat16), 'role', [(0, 1)])  11 us
    dot_general x5, matrix products, plain_training(): gradient = jnp.dot(own_inputs.T, slope, preferred_element_type=jnp.float32)  10.5 us
  transfers between devices with their start and end apart: 20, of which 14 were waited for; matrix products, arithmetic and copies ran while one was open for 13% of the time, Pallas kernels for 0%

profile of v1, /device:TPU:0, one launch (start us, length us, event | category | flops | bytes accessed | tf_op | source)
XLA Modules:
  0.0 473.2 jit_solution(4574734170872293664)
XLA Ops:
  7.2 2.3 bitcast_convert_fusion.1
  9.6 2.0 fusion.60
  14.2 3.8 bitcast_convert_fusion
  18.0 37.9 %all-gather.11.cloned.1.call-done = bf16[1,1024,1024]{2,1,0:T(8,128)(2,1)} async-done(((bf16[1,64,1024]{2,1,0:T(8,128)(2,1)}), bf16[1,1024,1024]{2,1,0:T(8,128)(2,1)}) %all-gather.11.cloned.1.call-update) | async-done | bytes 2097168 | tf_op jit(solution)/shard_map/all_gather | solution.py:52
  55.9 4.4 multiply_convert_fusion.10
  60.3 38.0 %all-gather.13.cloned.1.call-done = bf16[1,1024,1024]{2,1,0:T(8,128)(2,1)} async-done(((bf16[1,64,1024]{2,1,0:T(8,128)(2,1)}), bf16[1,1024,1024]{2,1,0:T(8,128)(2,1)}) %all-gather.13.cloned.1.call-update) | async-done | bytes 2097168 | tf_op jit(solution)/shard_map/all_gather | solution.py:52
  98.3 4.4 multiply_convert_fusion.9
  102.7 38.5 %all-gather.15.cloned.1.call-done = bf16[1,1024,1024]{2,1,0:T(8,128)(2,1)} async-done(((bf16[1,64,1024]{2,1,0:T(8,128)(2,1)}), bf16[1,1024,1024]{2,1,0:T(8,128)(2,1)}) %all-gather.15.cloned.1.call-update) | async-done | bytes 2097168 | tf_op jit(solution)/shard_map/all_gather | solution.py:52
  141.2 4.3 multiply_convert_fusion.8
  145.5 38.5 %all-gather.17.cloned.1.call-done = bf16[1,1024,1024]{2,1,0:T(8,128)(2,1)} async-done(((bf16[1,64,1024]{2,1,0:T(8,128)(2,1)}), bf16[1,1024,1024]{2,1,0:T(8,128)(2,1)}) %all-gather.17.cloned.1.call-update) | async-done | bytes 2097168 | tf_op jit(solution)/shard_map/all_gather | solution.py:52
  184.0 4.4 multiply_convert_fusion.7
  188.4 38.4 %all-gather.19.cloned.1.call-done = bf16[1,1024,1024]{2,1,0:T(8,128)(2,1)} async-done(((bf16[1,64,1024]{2,1,0:T(8,128)(2,1)}), bf16[1,1024,1024]{2,1,0:T(8,128)(2,1)}) %all-gather.19.cloned.1.call-update) | async-done | bytes 2097168 | tf_op jit(solution)/shard_map/all_gather | solution.py:52
  226.8 3.0 fusion.10
  229.8 3.7 multiply_convert_fusion.5
  233.5 2.9 fusion.64
  236.7 3.9 collective-permute-done.5
  241.7 47.2 %collective-permute-done.6 = f32[512,1024]{1,0:T(8,128)S(1)} collective-permute-done((f32[512,1024]{1,0:T(8,128)S(1)}, f32[512,1024]{1,0:T(8,128)S(1)}, u32[]{:S(2)}, u32[]{:S(2)}) %collective-permute-start.6) | collective-permute-done | bytes 2097184 | tf_op jit(solution)/shard_map/ppermute | solution.py:68
  289.9 4.8 %collective-permute-start.4 = (bf16[1024,1024]{1,0:T(8,128)(2,1)}, bf16[1024,1024]{1,0:T(8,128)(2,1)}, u32[]{:S(2)}, u32[]{:S(2)}) collective-permute-start(bf16[1024,1024]{1,0:T(8,128)(2,1)} %bitcast_convert_fusion), channel_id=1, source_target_pairs={{0,16},{1,17},{2,18},{3,19},{4,20},{5,21},{6,22},{7,23},{8,24},{9,... | collective-permute-start | bytes 6291464 | tf_op jit(solution)/shard_map/ppermute | solution.py:38
  294.7 4.1 collective-permute-start.1
  298.8 40.6 %collective-permute-done = f32[513,1]{1,0:T(8,128)S(1)} collective-permute-done((f32[513,1]{1,0:T(8,128)S(1)}, f32[513,1]{1,0:T(8,128)S(1)}, u32[]{:S(2)}, u32[]{:S(2)}) %collective-permute-start) | collective-permute-done | bytes 2084 | tf_op jit(solution)/shard_map/ppermute | solution.py:16
  339.6 4.0 fusion.61
  345.6 2.0 fusion.59
  347.7 6.1 %collective-permute-start.2 = (bf16[512,1024]{1,0:T(8,128)(2,1)S(1)}, bf16[512,1024]{1,0:T(8,128)(2,1)S(1)}, u32[]{:S(2)}, u32[]{:S(2)}) collective-permute-start(bf16[512,1024]{1,0:T(8,128)(2,1)S(1)} %get-tuple-element.5), channel_id=1, source_target_pairs={{0,16},{1,17},{2,18},{3,19},{4,20},{5,21},{6,22},{7,23},{8,24},{9,... | collective-permute-start | bytes 3145736 | tf_op jit(solution)/shard_map/ppermute | solution.py:38
  353.8 1.8 add.99
  355.6 2.2 collective-permute-start.14
  357.8 11.0 %collective-permute-done.2 = bf16[512,1024]{1,0:T(8,128)(2,1)S(1)} collective-permute-done((bf16[512,1024]{1,0:T(8,128)(2,1)S(1)}, bf16[512,1024]{1,0:T(8,128)(2,1)S(1)}, u32[]{:S(2)}, u32[]{:S(2)}) %collective-permute-start.2) | collective-permute-done | bytes 1048608 | tf_op jit(solution)/shard_map/ppermute | solution.py:38
  368.7 2.0 gather_fusion
  370.8 3.4 select_bitcast_fusion
  374.2 6.7 %fusion.1 = f32[1,1024,1024]{2,1,0:T(8,128)} fusion(f32[1024,1024]{1,0:T(8,128)} %get-tuple-element.23, f32[1,1024,1024]{2,1,0:T(8,128)S(1)} %copy-done.2, bf16[1024,1024]{1,0:T(8,128)(2,1)} %collective-permute-done.3, bf16[1024,1024]{1,0:T(8,128)(2,1)} %collective-permute-done.4, pred[]{:T(512)S(6)} %eq.4), kind=kLoop, calls=%fused_computation.4 | loop fusion | flops 9437184 | bytes 16777216 | tf_op jit(solution)/shard_map/broadcast_in_dim | solution.py:121
  380.8 49.2 %collective-permute-done.8 = f32[512,1024]{1,0:T(8,128)} collective-permute-done((f32[512,1024]{1,0:T(8,128)}, f32[512,1024]{1,0:T(8,128)}, u32[]{:S(2)}, u32[]{:S(2)}) %collective-permute-start.8) | collective-permute-done | bytes 2097184 | tf_op jit(solution)/shard_map/ppermute | solution.py:68
  430.0 3.3 multiply_convert_fusion.4
  433.4 1.7 multiply_convert_fusion.3
  435.6 1.6 multiply_convert_fusion.2
  437.8 2.6 multiply_convert_fusion.1
  440.4 4.3 bitcast_dynamic-update-slice_fusion.4
  444.8 1.8 bitcast_dynamic-update-slice_fusion.3
  446.5 1.3 collective-permute-start.10
  447.8 1.3 collective-permute-start.9
  449.1 1.7 bitcast_dynamic-update-slice_fusion.2
  450.9 1.3 collective-permute-start.11
  452.2 1.4 bitcast_dynamic-update-slice_fusion.1
  453.6 1.3 collective-permute-start.12
  454.9 1.3 bitcast_dynamic-update-slice_fusion
  456.2 1.4 collective-permute-done.9
  459.0 1.5 collective-permute-done.11
  460.4 2.8 collective-permute-done.12
  463.3 1.9 collective-permute-done.13
  465.1 1.6 fusion.35
  (80 shorter events, 9.7 us)
Async XLA Ops:
  7.2 48.7 %copy-start = (bf16[512,1024]{1,0:T(8,128)(2,1)S(1)}, bf16[512,1024]{1,0:T(8,128)(2,1)}, u32[]{:S(2)}) copy-start(bf16[512,1024]{1,0:T(8,128)(2,1)} %param.10) | copy-start | bytes 3145732
  7.2 48.7 %all-gather.11.cloned.1.call-start = ((), (), s32[]{:S(2)}) async-start(), calls=%async_computation | async-start | bytes 2228224 | tf_op jit(solution)/shard_map/all_gather | solution.py:52
  11.6 86.7 %all-gather.13.cloned.1.call-start = ((), (), s32[]{:S(2)}) async-start(), calls=%async_computation.1 | async-start | bytes 2228224 | tf_op jit(solution)/shard_map/all_gather | solution.py:52
  12.3 128.9 %all-gather.15.cloned.1.call-start = ((), (), s32[]{:S(2)}) async-start(), calls=%async_computation.2 | async-start | bytes 2228224 | tf_op jit(solution)/shard_map/all_gather | solution.py:52
  13.1 171.0 %all-gather.17.cloned.1.call-start = ((), (), s32[]{:S(2)}) async-start(), calls=%async_computation.3 | async-start | bytes 2228224 | tf_op jit(solution)/shard_map/all_gather | solution.py:52
  13.6 213.2 %all-gather.19.cloned.1.call-start = ((), (), s32[]{:S(2)}) async-start(), calls=%async_computation.4 | async-start | bytes 2228224 | tf_op jit(solution)/shard_map/all_gather | solution.py:52
  60.3 42.4 %copy-start.13 = (bf16[512,1024]{1,0:T(8,128)(2,1)}, bf16[512,1024]{1,0:T(8,128)(2,1)S(1)}, u32[]{:S(2)}) copy-start(bf16[512,1024]{1,0:T(8,128)(2,1)S(1)} %get-tuple-element.14) | copy-start | bytes 3145732
  102.7 42.8 %copy-start.12 = (bf16[512,1024]{1,0:T(8,128)(2,1)}, bf16[512,1024]{1,0:T(8,128)(2,1)S(1)}, u32[]{:S(2)}) copy-start(bf16[512,1024]{1,0:T(8,128)(2,1)S(1)} %get-tuple-element.16) | copy-start | bytes 3145732
  145.5 42.9 %copy-start.11 = (bf16[512,1024]{1,0:T(8,128)(2,1)}, bf16[512,1024]{1,0:T(8,128)(2,1)S(1)}, u32[]{:S(2)}) copy-start(bf16[512,1024]{1,0:T(8,128)(2,1)S(1)} %get-tuple-element.18) | copy-start | bytes 3145732
  188.4 41.4 %copy-start.10 = (bf16[512,1024]{1,0:T(8,128)(2,1)}, bf16[512,1024]{1,0:T(8,128)(2,1)S(1)}, u32[]{:S(2)}) copy-start(bf16[512,1024]{1,0:T(8,128)(2,1)S(1)} %get-tuple-element.20) | copy-start | bytes 3145732
  226.8 3.0 copy-start.1
  229.8 109.7 %copy-start.4 = (f32[512,1024]{1,0:T(8,128)}, f32[512,1024]{1,0:T(8,128)S(1)}, u32[]{:S(2)}) copy-start(f32[512,1024]{1,0:T(8,128)S(1)} %fusion.10) | copy-start | bytes 6291460
  236.4 4.2 collective-permute-start.5
  241.0 48.7 %copy-start.9 = (f32[1024]{0:T(1024)S(1)}, f32[1024]{0:T(1024)}, u32[]{:S(2)}) copy-start(f32[1024]{0:T(1024)} %param.8) | copy-start | bytes 12292
  241.0 47.8 %collective-permute-start.6 = (f32[512,1024]{1,0:T(8,128)S(1)}, f32[512,1024]{1,0:T(8,128)S(1)}, u32[]{:S(2)}, u32[]{:S(2)}) collective-permute-start(f32[512,1024]{1,0:T(8,128)S(1)} %add.97), channel_id=1, source_target_pairs={{0,2},{1,3},{2,0},{3,1},{4,6},{5,7},{6,4},{7,5},{8,10},{9,11},{10,... | collective-permute-start | bytes 6291464 | tf_op jit(solution)/shard_map/ppermute | solution.py:68
  289.3 64.5 %collective-permute-start.7 = (f32[512,1024]{1,0:T(8,128)S(1)}, f32[512,1024]{1,0:T(8,128)S(1)}, u32[]{:S(2)}, u32[]{:S(2)}) collective-permute-start(f32[512,1024]{1,0:T(8,128)S(1)} %add.98), channel_id=1, source_target_pairs={{0,4},{1,5},{2,6},{3,7},{4,0},{5,1},{6,2},{7,3},{8,12},{9,13},{10,... | collective-permute-start | bytes 6291464 | tf_op jit(solution)/shard_map/ppermute | solution.py:68
  289.9 49.6 %collective-permute-start = (f32[513,1]{1,0:T(8,128)S(1)}, f32[513,1]{1,0:T(8,128)S(1)}, u32[]{:S(2)}, u32[]{:S(2)}) collective-permute-start(f32[513,1]{1,0:T(8,128)S(1)} %get-tuple-element.7), channel_id=1, source_target_pairs={{0,1},{1,2},{2,3},{3,4},{4,5},{5,6},{6,7},{7,8},{8,9},{9,10},{10,1... | collective-permute-start | bytes 6164 | tf_op jit(solution)/shard_map/ppermute | solution.py:16
  289.9 84.2 %collective-permute-start.4 = (bf16[1024,1024]{1,0:T(8,128)(2,1)}, bf16[1024,1024]{1,0:T(8,128)(2,1)}, u32[]{:S(2)}, u32[]{:S(2)}) collective-permute-start(bf16[1024,1024]{1,0:T(8,128)(2,1)} %bitcast_convert_fusion), channel_id=1, source_target_pairs={{0,16},{1,17},{2,18},{3,19},{4,20},{5,21},{6,22},{7,23},{8,24},{9,... | collective-permute-start | bytes 6291464 | tf_op jit(solution)/shard_map/ppermute | solution.py:38
  294.7 50.2 %collective-permute-start.1 = (f32[513,1]{1,0:T(8,128)S(1)}, f32[513,1]{1,0:T(8,128)S(1)}, u32[]{:S(2)}, u32[]{:S(2)}) collective-permute-start(f32[513,1]{1,0:T(8,128)S(1)} %get-tuple-element.8), channel_id=1, source_target_pairs={{1,0},{2,1},{3,2},{4,3},{5,4},{6,5},{7,6},{8,7},{9,8},{10,9},{11,1... | collective-permute-start | bytes 6164 | tf_op jit(solution)/shard_map/ppermute | solution.py:17
  343.6 30.6 %collective-permute-start.3 = (bf16[1024,1024]{1,0:T(8,128)(2,1)}, bf16[1024,1024]{1,0:T(8,128)(2,1)}, u32[]{:S(2)}, u32[]{:S(2)}) collective-permute-start(bf16[1024,1024]{1,0:T(8,128)(2,1)} %get-tuple-element.22), channel_id=1, source_target_pairs={{16,0},{17,1},{18,2},{19,3},{20,4},{21,5},{22,6},{23,7},{24,8},{25... | collective-permute-start | bytes 6291464 | tf_op jit(solution)/shard_map/ppermute | solution.py:42
  344.9 0.7 copy-start.15
  347.7 10.1 %copy-start.14 = (s32[512]{0:T(512)S(1)}, s32[512]{0:T(512)}, u32[]{:S(2)}) copy-start(s32[512]{0:T(512)} %param.11) | copy-start | bytes 6148
  347.7 21.1 %collective-permute-start.2 = (bf16[512,1024]{1,0:T(8,128)(2,1)S(1)}, bf16[512,1024]{1,0:T(8,128)(2,1)S(1)}, u32[]{:S(2)}, u32[]{:S(2)}) collective-permute-start(bf16[512,1024]{1,0:T(8,128)(2,1)S(1)} %get-tuple-element.5), channel_id=1, source_target_pairs={{0,16},{1,17},{2,18},{3,19},{4,20},{5,21},{6,22},{7,23},{8,24},{9,... | collective-permute-start | bytes 3145736 | tf_op jit(solution)/shard_map/ppermute | solution.py:38
  355.6 74.5 %collective-permute-start.8 = (f32[512,1024]{1,0:T(8,128)}, f32[512,1024]{1,0:T(8,128)}, u32[]{:S(2)}, u32[]{:S(2)}) collective-permute-start(f32[512,1024]{1,0:T(8,128)} %add.99), channel_id=1, source_target_pairs={{0,8},{1,9},{2,10},{3,11},{4,12},{5,13},{6,14},{7,15},{8,0},{9,1},... | collective-permute-start | bytes 6291464 | tf_op jit(solution)/shard_map/ppermute | solution.py:68
  355.6 109.6 %collective-permute-start.14 = (bf16[5,64,1024]{2,1,0:T(8,128)(2,1)}, bf16[5,64,1024]{2,1,0:T(8,128)(2,1)}, u32[]{:S(2)}, u32[]{:S(2)}) collective-permute-start(bf16[5,64,1024]{2,1,0:T(8,128)(2,1)} %bitcast_convert_fusion.1), channel_id=1, source_target_pairs={{0,16},{1,17},{2,18},{3,19},{4,20},{5,21},{6,22},{7,23},{8,24},{9,... | collective-permute-start | bytes 1966088 | tf_op jit(solution)/shard_map/ppermute | solution.py:38
  370.8 3.4 copy-start.2
  374.2 55.9 %copy-start.5 = (f32[512,1024]{1,0:T(8,128)S(1)}, f32[512,1024]{1,0:T(8,128)}, u32[]{:S(2)}) copy-start(f32[512,1024]{1,0:T(8,128)} %copy-done.4) | copy-start | bytes 6291460
  380.8 52.5 %copy-start.18 = (bf16[1,1024,1024]{2,1,0:T(8,128)(2,1)S(1)}, bf16[1,1024,1024]{2,1,0:T(8,128)(2,1)}, u32[]{:S(2)}) copy-start(bf16[1,1024,1024]{2,1,0:T(8,128)(2,1)} %all-gather.19.cloned.1.call-done) | copy-start | bytes 6291460
  380.8 52.5 %copy-start.21 = (f32[512,1024]{1,0:T(8,128)S(1)}, f32[512,1024]{1,0:T(8,128)}, u32[]{:S(2)}) copy-start(f32[512,1024]{1,0:T(8,128)} %get-tuple-element.21) | copy-start | bytes 6291460
  433.4 1.7 copy-start.17
  433.4 2.2 copy-start.20
  435.1 2.2 copy-start.6
  435.6 1.7 copy-start.16
  435.6 2.2 copy-start.19
  437.3 3.2 copy-start.8
  444.8 7.4 %copy-start.7 = (bf16[512,1024]{1,0:T(8,128)(2,1)S(1)}, bf16[512,1024]{1,0:T(8,128)(2,1)}, u32[]{:S(2)}) copy-start(bf16[512,1024]{1,0:T(8,128)(2,1)} %copy-done.6) | copy-start | bytes 3145732
  446.5 12.4 %collective-permute-start.10 = (bf16[64,1024]{1,0:T(8,128)(2,1)S(1)}, bf16[64,1024]{1,0:T(8,128)(2,1)S(1)}, u32[]{:S(2)}, u32[]{:S(2)}) collective-permute-start(bf16[64,1024]{1,0:T(8,128)(2,1)S(1)} %get-tuple-element.27), channel_id=1, source_target_pairs={{16,0},{17,1},{18,2},{19,3},{20,4},{21,5},{22,6},{23,7},{24,8},{25... | collective-permute-start | bytes 393224 | tf_op jit(solution)/shard_map/ppermute | solution.py:42
  447.8 9.8 %collective-permute-start.9 = (bf16[64,1024]{1,0:T(8,128)(2,1)S(1)}, bf16[64,1024]{1,0:T(8,128)(2,1)S(1)}, u32[]{:S(2)}, u32[]{:S(2)}) collective-permute-start(bf16[64,1024]{1,0:T(8,128)(2,1)S(1)} %get-tuple-element.25), channel_id=1, source_target_pairs={{16,0},{17,1},{18,2},{19,3},{20,4},{21,5},{22,6},{23,7},{24,8},{25... | collective-permute-start | bytes 393224 | tf_op jit(solution)/shard_map/ppermute | solution.py:42
  450.9 9.6 %collective-permute-start.11 = (bf16[64,1024]{1,0:T(8,128)(2,1)S(1)}, bf16[64,1024]{1,0:T(8,128)(2,1)S(1)}, u32[]{:S(2)}, u32[]{:S(2)}) collective-permute-start(bf16[64,1024]{1,0:T(8,128)(2,1)S(1)} %get-tuple-element.29), channel_id=1, source_target_pairs={{16,0},{17,1},{18,2},{19,3},{20,4},{21,5},{22,6},{23,7},{24,8},{25... | collective-permute-start | bytes 393224 | tf_op jit(solution)/shard_map/ppermute | solution.py:42
  452.2 13.0 %copy-start.3 = (f32[1,5,64,1024]{3,2,1,0:T(8,128)S(1)}, f32[1,5,64,1024]{3,2,1,0:T(8,128)}, u32[]{:S(2)}) copy-start(f32[1,5,64,1024]{3,2,1,0:T(8,128)} %param.13) | copy-start | bytes 3932164
  453.6 9.6 %collective-permute-start.12 = (bf16[64,1024]{1,0:T(8,128)(2,1)S(1)}, bf16[64,1024]{1,0:T(8,128)(2,1)S(1)}, u32[]{:S(2)}, u32[]{:S(2)}) collective-permute-start(bf16[64,1024]{1,0:T(8,128)(2,1)S(1)} %get-tuple-element.31), channel_id=1, source_target_pairs={{16,0},{17,1},{18,2},{19,3},{20,4},{21,5},{22,6},{23,7},{24,8},{25... | collective-permute-start | bytes 393224 | tf_op jit(solution)/shard_map/ppermute | solution.py:42
  457.6 7.5 %collective-permute-start.13 = (bf16[64,1024]{1,0:T(8,128)(2,1)S(1)}, bf16[64,1024]{1,0:T(8,128)(2,1)S(1)}, u32[]{:S(2)}, u32[]{:S(2)}) collective-permute-start(bf16[64,1024]{1,0:T(8,128)(2,1)S(1)} %get-tuple-element.33), channel_id=1, source_target_pairs={{16,0},{17,1},{18,2},{19,3},{20,4},{21,5},{22,6},{23,7},{24,8},{25... | collective-permute-start | bytes 393224 | tf_op jit(solution)/shard_map/ppermute | solution.py:42
Sparse Core Ops, SparseCore 0:
  11.7 44.1 all-gather.10
  58.1 40.1 all-gather.12
  101.0 40.1 all-gather.14
  143.8 40.1 all-gather.16
  186.6 40.1 all-gather.18
